TPU v7x, 512 devices: a whole 4x8x8 slice. The times are simulated.
512 devices in a mesh: dom: 32 (over y, x_hi, core), band: 16 (over z, x_lo).
Axes of the slice: x: 4 (x_hi: 2, x_lo: 2; x = x_hi * 2 + x_lo), y: 8, z: 8, core: 2. Of those that a mesh axis runs over, the one named last changes fastest.
Arguments:
- psi: float32 [512, 192, 512], P('band', 'dom'), may hold values from -40 to 40, as said below
- potential: float32 [192, 512], P('dom'), may hold values from -3 to 1
Outputs:
- filtered_basis: float32 [512, 192, 512], P('band', 'dom')
Inputs may be any that keep to these rules, and one draw needn't show every extreme that they name: `psi`: real-valued band functions.
All inputs are finite; a program needn't handle non-finite values.
Results may differ from a plain program's by a relative error of at most 0.0002.
Values sent between devices are 32-bit elements; how exact they have to be, the bound alone decides.
No kernel may reach another device: no remote copies, remote signals or barrier semaphores. Data moves between devices by JAX's collectives and lax.ppermute only.
A program may use at most 64 MiB of HBM per device.

v0:
```python
import jax
import jax.numpy as jnp
from jax import lax
from jax.sharding import PartitionSpec as P

LX = 32
DEG = 4
COEF = (
    -5369.0 / 1800.0,
    12.0 / 7.0,
    -15.0 / 56.0,
    10.0 / 189.0,
    -1.0 / 112.0,
    2.0 / 1925.0,
    -1.0 / 16632.0,
)
INV_SPACING2 = 4.0
CENTRE = 24.0
HALF_WIDTH = 20.0


def with_halo(block, sides, width):
    for axis, dim in sides:
        count = lax.axis_size(axis)
        forward = [(i, i + 1) for i in range(count - 1)]
        backward = [(target, source) for source, target in forward]
        low = lax.ppermute(
            lax.slice_in_dim(block, block.shape[dim] - width, None, axis=dim), axis, forward
        )
        high = lax.ppermute(lax.slice_in_dim(block, 0, width, axis=dim), axis, backward)
        block = jnp.concatenate([low, block, high], axis=dim)
    return block


def shift_x(values, step):
    amount = step % LX
    column = lax.broadcasted_iota(jnp.int32, values.shape, 2) % LX
    return jnp.where(
        column >= amount, jnp.roll(values, amount, 2), jnp.roll(values, amount - LX, 2)
    )


def shift_y(values, step):
    return jnp.roll(values, step * LX, 2)


def hamiltonian(values, potential):
    depth = values.shape[1]
    padded = with_halo(values, (("dom", 1),), 6)
    summed = 3.0 * COEF[0] * values
    for step in range(1, 7):
        beside_all = shift_x(values, step) + shift_x(values, -step)
        beside_all = beside_all + shift_y(values, step) + shift_y(values, -step)
        beside_all = (
            beside_all
            + padded[:, 6 + step : 6 + step + depth]
            + padded[:, 6 - step : 6 - step + depth]
        )
        summed = summed + COEF[step] * beside_all
    return -0.5 * INV_SPACING2 * summed + potential[None] * values


def chebyshev(start, potential):
    previous = start
    current = (hamiltonian(start, potential) - CENTRE * start) / HALF_WIDTH
    for degree in range(1, DEG):
        following = (
            2.0 * (hamiltonian(current, potential) - CENTRE * current) / HALF_WIDTH - previous
        )
        previous, current = (current, following)
    return current


def inverse_rows(gram, all_bands, tile_bands):
    lower = jnp.linalg.cholesky(gram)
    inverse = lax.linalg.triangular_solve(
        lower, jnp.eye(all_bands, dtype=jnp.float32), left_side=True, lower=True
    )
    return lax.dynamic_slice_in_dim(inverse, lax.axis_index("band") * tile_bands, tile_bands, 0)


def shards(psi, potential):
    filtered = chebyshev(psi, potential)
    tile_bands = psi.shape[0]
    points_dev = psi.shape[1] * psi.shape[2]
    all_points = points_dev * lax.axis_size("dom")
    all_bands = tile_bands * lax.axis_size("band")
    flatrows = filtered.reshape(tile_bands, points_dev)
    piece = lax.all_gather(filtered, "band", axis=0, tiled=True)
    count = piece.shape[0]
    contrib = jnp.dot(
        flatrows,
        piece.reshape(count, points_dev).T,
        precision=lax.Precision.HIGHEST,
        preferred_element_type=jnp.float32,
    )
    gram_rows = lax.psum(contrib, "dom") / all_points
    gram = lax.all_gather(gram_rows, "band", axis=0, tiled=True)
    my_rows = inverse_rows(gram, all_bands, tile_bands)
    piece = lax.all_gather(filtered, "band", axis=0, tiled=True)
    count = piece.shape[0]
    rotated = jnp.dot(
        my_rows,
        piece.reshape(count, points_dev),
        precision=lax.Precision.HIGHEST,
        preferred_element_type=jnp.float32,
    )
    return rotated.reshape(psi.shape)


def solution(mesh):
    placed = (P("band", "dom", None), P("dom", None))
    return jax.shard_map(
        shards, mesh=mesh, in_specs=placed, out_specs=P("band", "dom", None), check_vma=False
    )
```

profile of v0, /device:TPU:6, one launch (start us, length us, event | category | flops | bytes accessed | tf_op | source)
XLA Modules:
  0.0 725.2 jit_solution(7436480236359161126)
XLA Ops:
  6.5 2.0 collective-permute-start.1
  8.6 5.1 collective-permute-start
  23.2 3.9 broadcast_multiply_fusion
  31.5 1.9 collective-permute-start.2
  33.4 2.6 collective-permute-start.3
  36.3 2.4 collective-permute-done.2
  38.7 8.4 %collective-permute-done.3 = f32[32,6,512]{2,0,1:T(8,128)S(1)} collective-permute-done((f32[32,6,512]{2,0,1:T(8,128)S(1)}, f32[32,6,512]{2,0,1:T(8,128)S(1)}, u32[]{:S(2)}, u32[]{:S(2)}) %collective-permute-start.3) | collective-permute-done | bytes 393248 | tf_op jit(solution)/shard_map/ppermute | solution.py:27
  47.1 3.8 fusion.80
  53.7 1.9 collective-permute-start.4
  55.6 2.4 collective-permute-start.5
  60.9 6.2 collective-permute-done.5
  67.1 3.8 fusion.92
  73.7 1.9 collective-permute-start.6
  75.7 2.8 collective-permute-start.7
  80.9 6.3 collective-permute-done.7
  87.3 4.5 fusion.104
  91.8 150.9 %all-gather.3.cloned.1.call-done = f32[512,6,512]{2,0,1:T(8,128)} async-done(((f32[32,6,512]{2,0,1:T(8,128)}), f32[512,6,512]{2,0,1:T(8,128)}) %all-gather.3.cloned.1.call-update) | async-done | bytes 6291472 | tf_op jit(solution)/shard_map/all_gather | solution.py:89
  242.7 9.3 %convolution_bitcast_fusion = f32[32,512]{1,0:T(8,128)} fusion(f32[32,6,512]{2,0,1:T(8,128)} %fusion.104, f32[512,6,512]{2,0,1:T(8,128)} %all-gather.3.cloned.1.call-done), kind=kOutput, calls=%fused_computation.72 | convolution fusion | flops 603979776 | bytes 6750208 | tf_op jit(solution)/shard_map/dot_general | solution.py:91
  252.0 242.1 %all-reduce.3.cloned.1.call-done = f32[32,512]{1,0:T(8,128)} async-done(((f32[32,512]{1,0:T(8,128)}), f32[32,512]{1,0:T(8,128)}) %all-reduce.3.cloned.1.call-update) | async-done | bytes 65552 | tf_op jit(solution)/shard_map/psum | solution.py:97
  496.6 6.7 copy.9
  503.3 65.1 %all-gather.5.cloned.1.call-done = f32[512,512]{1,0:T(8,128)} async-done(((f32[32,512]{1,0:T(8,128)}), f32[512,512]{1,0:T(8,128)}) %all-gather.5.cloned.1.call-update) | async-done | bytes 1048592 | tf_op jit(solution)/shard_map/all_gather | solution.py:98
  571.4 11.7 %cholesky.104 = f32[128,128]{1,0:T(8,128)S(1)} custom-call(f32[128,128]{1,0:T(8,128)S(1)} %cholesky.266), custom_call_target="Cholesky" | custom-call | tf_op jit(solution)/shard_map/jit(cholesky)/cholesky | solution.py:75
  583.3 9.8 %custom-call.30 = f32[1,128,128]{1,2,0:T(8,128)S(1)} custom-call(f32[1,128,128]{2,1,0:T(8,128)S(1)} %get-tuple-element.324), custom_call_target="InvertDiagBlocksLowerTriangular" | custom-call | tf_op jit(solution)/shard_map/jit(cholesky)/cholesky | solution.py:75
  593.8 11.7 %cholesky.217 = f32[128,128]{1,0:T(8,128)S(1)} custom-call(f32[128,128]{1,0:T(8,128)S(1)} %cholesky.270), custom_call_target="Cholesky" | custom-call | tf_op jit(solution)/shard_map/jit(cholesky)/cholesky | solution.py:75
  605.5 10.0 %custom-call.31 = f32[1,128,128]{1,2,0:T(8,128)S(1)} custom-call(f32[1,128,128]{2,1,0:T(8,128)S(1)} %get-tuple-element.321), custom_call_target="InvertDiagBlocksLowerTriangular" | custom-call | tf_op jit(solution)/shard_map/jit(cholesky)/cholesky | solution.py:75
  616.2 11.7 %cholesky.238 = f32[128,128]{1,0:T(8,128)S(1)} custom-call(f32[128,128]{1,0:T(8,128)S(1)} %cholesky.275), custom_call_target="Cholesky" | custom-call | tf_op jit(solution)/shard_map/jit(cholesky)/cholesky | solution.py:75
  628.5 9.8 %custom-call.32 = f32[1,128,128]{1,2,0:T(8,128)S(1)} custom-call(f32[1,128,128]{2,1,0:T(8,128)S(1)} %get-tuple-element.318), custom_call_target="InvertDiagBlocksLowerTriangular" | custom-call | tf_op jit(solution)/shard_map/jit(cholesky)/cholesky | solution.py:75
  639.0 11.7 %cholesky.255 = f32[128,128]{1,0:T(8,128)S(1)} custom-call(f32[128,128]{1,0:T(8,128)S(1)} %convolution_subtract_fusion.5), custom_call_target="Cholesky" | custom-call | tf_op jit(solution)/shard_map/jit(cholesky)/cholesky | solution.py:75
  654.7 10.3 %while.1 = (s32[]{:T(128)}, f32[512,512]{1,0:T(8,128)S(1)}, s32[4,2]{0,1:T(2,128)S(1)}, f32[4,128,128]{2,1,0:T(8,128)}, s32[]{:T(128)}) while((s32[]{:T(128)}, f32[512,512]{1,0:T(8,128)S(1)}, s32[4,2]{0,1:T(2,128)S(1)}, f32[4,128,128]{2,1,0:T(8,128)}, s32[]{:T(128)}) %tuple.173), condition=%wide.while_cond, body=%wide.while_body.sunk | while | flops 2 | bytes 132705 | solution.py:76
  658.1 1.9 bitcast_dynamic-update-slice_fusion.2
  665.0 40.1 %custom-call.33 = f32[4,128,128]{1,2,0:T(8,128)S(1)} custom-call(f32[4,128,128]{2,1,0:T(8,128)} %get-tuple-element.12), custom_call_target="InvertDiagBlocksLowerTriangular" | custom-call | tf_op jit(solution)/shard_map/triangular_solve | solution.py:76
  709.0 9.2 %fusion = f32[32,6,512]{2,0,1:T(8,128)} fusion(f32[512,6,512]{0,2,1:T(8,128)} %copy.9, s32[]{:T(128)S(6)} %select_n.397, f32[128,512]{1,0:T(8,128)S(1)} %fusion.271, f32[128,512]{1,0:T(8,128)S(1)} %fusion.286, f32[128,512]{1,0:T(8,128)S(1)} %fusion.284, f32[128,512]{1,0:T(8,128)S(1)} %fusion.283), kind=kOutput, calls=%fused_computation.2 | convolution fusion | flops 604028928 | bytes 7733252 | tf_op jit(solution)/shard_map/dot_general | solution.py:102
  (209 shorter events, 46.1 us)
Async XLA Ops:
  6.5 12.4 %copy-start = (f32[32,6,512]{2,0,1:T(8,128)S(1)}, f32[32,6,512]{2,0,1:T(8,128)}, u32[]{:S(2)}) copy-start(f32[32,6,512]{2,0,1:T(8,128)} %param.2) | copy-start | bytes 1179652
  6.5 236.2 %all-gather.3.cloned.1.call-start = ((), (), s32[]{:S(2)}) async-start(), calls=%async_computation | async-start | bytes 6684672 | tf_op jit(solution)/shard_map/all_gather | solution.py:89
  6.5 16.4 %collective-permute-start.1 = (f32[32,6,512]{2,0,1:T(8,128)}, f32[32,6,512]{2,0,1:T(8,128)S(1)}, u32[]{:S(2)}, u32[]{:S(2)}) collective-permute-start(f32[32,6,512]{2,0,1:T(8,128)} %param.2), channel_id=1, source_target_pairs={{0,16},{16,32},{32,48},{48,64},{64,80},{80,96},{96,112},{112,128},... | collective-permute-start | bytes 1179656 | tf_op jit(solution)/shard_map/ppermute | solution.py:27
  8.6 14.5 %collective-permute-start = (f32[32,6,512]{2,0,1:T(8,128)}, f32[32,6,512]{2,0,1:T(8,128)S(1)}, u32[]{:S(2)}, u32[]{:S(2)}) collective-permute-start(f32[32,6,512]{2,0,1:T(8,128)} %param.2), channel_id=1, source_target_pairs={{16,0},{32,16},{48,32},{64,48},{80,64},{96,80},{112,96},{128,112},... | collective-permute-start | bytes 1179656 | tf_op jit(solution)/shard_map/ppermute | solution.py:30
  20.7 2.2 copy-start.1
  31.5 7.2 collective-permute-start.2
  33.4 13.7 %collective-permute-start.3 = (f32[32,6,512]{2,0,1:T(8,128)S(1)}, f32[32,6,512]{2,0,1:T(8,128)S(1)}, u32[]{:S(2)}, u32[]{:S(2)}) collective-permute-start(f32[32,6,512]{2,0,1:T(8,128)S(1)} %get-tuple-element.21), channel_id=1, source_target_pairs={{0,16},{16,32},{32,48},{48,64},{64,80},{80,96},{96,112},{112,128},... | collective-permute-start | bytes 1179656 | tf_op jit(solution)/shard_map/ppermute | solution.py:27
  53.7 7.2 collective-permute-start.4
  55.6 11.5 %collective-permute-start.5 = (f32[32,6,512]{2,0,1:T(8,128)S(1)}, f32[32,6,512]{2,0,1:T(8,128)S(1)}, u32[]{:S(2)}, u32[]{:S(2)}) collective-permute-start(f32[32,6,512]{2,0,1:T(8,128)S(1)} %fusion.80), channel_id=1, source_target_pairs={{0,16},{16,32},{32,48},{48,64},{64,80},{80,96},{96,112},{112,128},... | collective-permute-start | bytes 1179656 | tf_op jit(solution)/shard_map/ppermute | solution.py:27
  73.7 7.2 collective-permute-start.6
  75.7 11.6 %collective-permute-start.7 = (f32[32,6,512]{2,0,1:T(8,128)S(1)}, f32[32,6,512]{2,0,1:T(8,128)S(1)}, u32[]{:S(2)}, u32[]{:S(2)}) collective-permute-start(f32[32,6,512]{2,0,1:T(8,128)S(1)} %fusion.92), channel_id=1, source_target_pairs={{0,16},{16,32},{32,48},{48,64},{64,80},{80,96},{96,112},{112,128},... | collective-permute-start | bytes 1179656 | tf_op jit(solution)/shard_map/ppermute | solution.py:27
  91.7 402.4 %all-reduce.3.cloned.1.call-start = ((), (), s32[]{:S(2)}) async-start(), calls=%async_computation.1 | async-start | bytes 131072 | tf_op jit(solution)/shard_map/psum | solution.py:97
  252.0 316.4 %all-gather.5.cloned.1.call-start = ((), (), s32[]{:S(2)}) async-start(), calls=%async_computation.2 | async-start | bytes 1114112 | tf_op jit(solution)/shard_map/all_gather | solution.py:98
Sparse Core Ops, SparseCore 0:
  91.9 150.8 all-gather.2
  252.1 241.9 all-reduce.2
  496.2 72.0 all-gather.4
where the time goes:
time: 732 us; the launch traced here: 725 us
  waiting for transfers between devices  483 us (66%)
  other arithmetic  139 us (19%)
  local copies, waits for them, and re-layouts  41.3 us (6%)
  matrix products  24.1 us (3%)
  starting transfers between devices  20.9 us (3%)
  between operations  17 us (2%)
    psum x1, waiting for transfers between devices, shards(): gram_rows = lax.psum(contrib, 'dom') / all_points  242 us
    all_gather x1, waiting for transfers between devices, shards(): piece = lax.all_gather(filtered, 'band', axis=0, tiled=True)  151 us
    another operation x14, other arithmetic, inverse_rows(): lower = jnp.linalg.cholesky(gram)  78.6 us
    all_gather x1, waiting for transfers between devices, shards(): gram = lax.all_gather(gram_rows, 'band', axis=0, tiled=True)  65.1 us
    another operation x3, other arithmetic, inverse_rows(): lax.linalg.triangular_solve(lower, jnp.eye(all_bands, dtype=jnp.float32),...  40.3 us
    ppermute x4, waiting for transfers between devices, with_halo(): lax.ppermute(lax.slice_in_dim(block, block.shape[dim] - width, None, axis...  20.9 us
  transfers between devices with their start and end apart: 11, of which 9 were waited for; matrix products, arithmetic and copies ran while one was open for 3% of the time, Pallas kernels for 0%

commit v1 on v0

--- a/solution.py
+++ b/solution.py
@@ -94,7 +94,7 @@
         precision=lax.Precision.HIGHEST,
         preferred_element_type=jnp.float32,
     )
-    gram_rows = lax.psum(contrib, "dom") / all_points
+    gram_rows = jnp.sum(lax.all_gather(contrib, "dom"), axis=0) / all_points
     gram = lax.all_gather(gram_rows, "band", axis=0, tiled=True)
     my_rows = inverse_rows(gram, all_bands, tile_bands)
     piece = lax.all_gather(filtered, "band", axis=0, tiled=True)

time: 732 us -> 573 us (0.78)
  waiting for transfers between devices: 483 us -> 324 us
    psum x1 -> x0, waiting for transfers between devices: 242 us -> none  [shards(): gram_rows = lax.psum(contrib, 'dom') / all_points]
    all_gather x0 -> x1, waiting for transfers between devices: none -> 84.9 us  [shards(): gram_rows = jnp.sum(lax.all_gather(contrib, 'dom'), axis=0) / all_points]
  transfers between devices with their start and end apart: 11 -> 11, of which waited for: 9 -> 9; matrix products, arithmetic and copies ran while one was open for 3% -> 4% of each run, Pallas kernels for 0% -> 0%
where the time goes in v1:
time: 573 us; the launch traced here: 567 us
  waiting for transfers between devices  324 us (57%)
  other arithmetic  139 us (24%)
  local copies, waits for them, and re-layouts  41.3 us (7%)
  matrix products  24.1 us (4%)
  starting transfers between devices  20.9 us (4%)
  between operations  17 us (3%)
    all_gather x1, waiting for transfers between devices, shards(): piece = lax.all_gather(filtered, 'band', axis=0, tiled=True)  151 us
    all_gather x1, waiting for transfers between devices, shards(): gram_rows = jnp.sum(lax.all_gather(contrib, 'dom'), axis=0) / all_points  84.9 us
    another operation x14, other arithmetic, inverse_rows(): lower = jnp.linalg.cholesky(gram)  78.6 us
    all_gather x1, waiting for transfers between devices, shards(): gram = lax.all_gather(gram_rows, 'band', axis=0, tiled=True)  62.8 us
    another operation x3, other arithmetic, inverse_rows(): lax.linalg.triangular_solve(lower, jnp.eye(all_bands, dtype=jnp.float32),...  40.3 us
    ppermute x4, waiting for transfers between devices, with_halo(): lax.ppermute(lax.slice_in_dim(block, block.shape[dim] - width, None, axis...  20.9 us
    sub x3, other arithmetic, chebyshev(): 2.0 * (hamiltonian(current, potential) - CENTRE * current) / HALF_WIDTH  12 us
  transfers between devices with their start and end apart: 11, of which 9 were waited for; matrix products, arithmetic and copies ran while one was open for 4% of the time, Pallas kernels for 0%

profile of v1, /device:TPU:6, one launch (start us, length us, event | category | flops | bytes accessed | tf_op | source)
XLA Modules:
  0.0 566.7 jit_solution(12525462955464050669)
XLA Ops:
  6.5 2.0 collective-permute-start.1
  8.6 5.1 collective-permute-start
  23.2 3.9 broadcast_multiply_fusion
  31.5 1.9 collective-permute-start.2
  33.4 2.6 collective-permute-start.3
  36.3 2.4 collective-permute-done.2
  38.7 8.4 %collective-permute-done.3 = f32[32,6,512]{2,0,1:T(8,128)S(1)} collective-permute-done((f32[32,6,512]{2,0,1:T(8,128)S(1)}, f32[32,6,512]{2,0,1:T(8,128)S(1)}, u32[]{:S(2)}, u32[]{:S(2)}) %collective-permute-start.3) | collective-permute-done | bytes 393248 | tf_op jit(solution)/shard_map/ppermute | solution.py:27
  47.1 3.8 fusion.80
  53.7 1.9 collective-permute-start.4
  55.6 2.4 collective-permute-start.5
  60.9 6.2 %collective-permute-done.5 = f32[32,6,512]{2,0,1:T(8,128)S(1)} collective-permute-done((f32[32,6,512]{2,0,1:T(8,128)S(1)}, f32[32,6,512]{2,0,1:T(8,128)S(1)}, u32[]{:S(2)}, u32[]{:S(2)}) %collective-permute-start.5) | collective-permute-done | bytes 393248 | tf_op jit(solution)/shard_map/ppermute | solution.py:27
  67.1 3.8 fusion.92
  73.7 1.9 collective-permute-start.6
  75.7 2.8 collective-permute-start.7
  80.9 6.3 %collective-permute-done.7 = f32[32,6,512]{2,0,1:T(8,128)S(1)} collective-permute-done((f32[32,6,512]{2,0,1:T(8,128)S(1)}, f32[32,6,512]{2,0,1:T(8,128)S(1)}, u32[]{:S(2)}, u32[]{:S(2)}) %collective-permute-start.7) | collective-permute-done | bytes 393248 | tf_op jit(solution)/shard_map/ppermute | solution.py:27
  87.3 4.5 fusion.104
  91.8 150.9 %all-gather.5.cloned.1.call-done = f32[512,6,512]{2,0,1:T(8,128)} async-done(((f32[32,6,512]{2,0,1:T(8,128)}), f32[512,6,512]{2,0,1:T(8,128)}) %all-gather.5.cloned.1.call-update) | async-done | bytes 6291472 | tf_op jit(solution)/shard_map/all_gather | solution.py:89
  242.7 9.3 %convolution_bitcast_fusion = f32[32,512]{1,0:T(8,128)} fusion(f32[32,6,512]{2,0,1:T(8,128)} %fusion.104, f32[512,6,512]{2,0,1:T(8,128)} %all-gather.5.cloned.1.call-done), kind=kOutput, calls=%fused_computation.72 | convolution fusion | flops 603979776 | bytes 6750208 | tf_op jit(solution)/shard_map/dot_general | solution.py:91
  252.1 84.9 %all-gather.9.cloned.1.call-done = f32[1024,512]{1,0:T(8,128)} async-done(((f32[32,512]{1,0:T(8,128)}), f32[1024,512]{1,0:T(8,128)}) %all-gather.9.cloned.1.call-update) | async-done | bytes 2097168 | tf_op jit(solution)/shard_map/all_gather | solution.py:97
  340.3 6.7 %copy.7 = f32[512,6,512]{0,2,1:T(8,128)} copy(f32[512,6,512]{2,0,1:T(8,128)} %all-gather.5.cloned.1.call-done) | data formatting | bytes 12582912 | tf_op jit(solution)/shard_map/all_gather | solution.py:89
  347.0 62.8 %all-gather.7.cloned.1.call-done = f32[512,512]{1,0:T(8,128)} async-done(((f32[32,512]{1,0:T(8,128)}), f32[512,512]{1,0:T(8,128)}) %all-gather.7.cloned.1.call-update) | async-done | bytes 1048592 | tf_op jit(solution)/shard_map/all_gather | solution.py:98
  412.9 11.7 %cholesky.104 = f32[128,128]{1,0:T(8,128)S(1)} custom-call(f32[128,128]{1,0:T(8,128)S(1)} %cholesky.266), custom_call_target="Cholesky" | custom-call | tf_op jit(solution)/shard_map/jit(cholesky)/cholesky | solution.py:75
  424.7 9.8 %custom-call.30 = f32[1,128,128]{1,2,0:T(8,128)S(1)} custom-call(f32[1,128,128]{2,1,0:T(8,128)S(1)} %get-tuple-element.324), custom_call_target="InvertDiagBlocksLowerTriangular" | custom-call | tf_op jit(solution)/shard_map/jit(cholesky)/cholesky | solution.py:75
  435.2 11.7 %cholesky.217 = f32[128,128]{1,0:T(8,128)S(1)} custom-call(f32[128,128]{1,0:T(8,128)S(1)} %cholesky.270), custom_call_target="Cholesky" | custom-call | tf_op jit(solution)/shard_map/jit(cholesky)/cholesky | solution.py:75
  447.0 10.0 %custom-call.31 = f32[1,128,128]{1,2,0:T(8,128)S(1)} custom-call(f32[1,128,128]{2,1,0:T(8,128)S(1)} %get-tuple-element.321), custom_call_target="InvertDiagBlocksLowerTriangular" | custom-call | tf_op jit(solution)/shard_map/jit(cholesky)/cholesky | solution.py:75
  457.6 11.7 %cholesky.238 = f32[128,128]{1,0:T(8,128)S(1)} custom-call(f32[128,128]{1,0:T(8,128)S(1)} %cholesky.275), custom_call_target="Cholesky" | custom-call | tf_op jit(solution)/shard_map/jit(cholesky)/cholesky | solution.py:75
  470.0 9.8 %custom-call.32 = f32[1,128,128]{1,2,0:T(8,128)S(1)} custom-call(f32[1,128,128]{2,1,0:T(8,128)S(1)} %get-tuple-element.318), custom_call_target="InvertDiagBlocksLowerTriangular" | custom-call | tf_op jit(solution)/shard_map/jit(cholesky)/cholesky | solution.py:75
  480.4 11.7 %cholesky.255 = f32[128,128]{1,0:T(8,128)S(1)} custom-call(f32[128,128]{1,0:T(8,128)S(1)} %convolution_subtract_fusion.5), custom_call_target="Cholesky" | custom-call | tf_op jit(solution)/shard_map/jit(cholesky)/cholesky | solution.py:75
  496.2 10.3 %while.1 = (s32[]{:T(128)}, f32[512,512]{1,0:T(8,128)S(1)}, s32[4,2]{0,1:T(2,128)S(1)}, f32[4,128,128]{2,1,0:T(8,128)}, s32[]{:T(128)}) while((s32[]{:T(128)}, f32[512,512]{1,0:T(8,128)S(1)}, s32[4,2]{0,1:T(2,128)S(1)}, f32[4,128,128]{2,1,0:T(8,128)}, s32[]{:T(128)}) %tuple.173), condition=%wide.while_cond, body=%wide.while_body.sunk | while | flops 2 | bytes 132705 | solution.py:76
  499.6 1.9 bitcast_dynamic-update-slice_fusion.2
  506.5 40.1 %custom-call.33 = f32[4,128,128]{1,2,0:T(8,128)S(1)} custom-call(f32[4,128,128]{2,1,0:T(8,128)} %get-tuple-element.12), custom_call_target="InvertDiagBlocksLowerTriangular" | custom-call | tf_op jit(solution)/shard_map/triangular_solve | solution.py:76
  550.5 9.2 %fusion = f32[32,6,512]{2,0,1:T(8,128)} fusion(f32[512,6,512]{0,2,1:T(8,128)} %copy.7, s32[]{:T(128)S(6)} %select_n.397, f32[128,512]{1,0:T(8,128)S(1)} %fusion.271, f32[128,512]{1,0:T(8,128)S(1)} %fusion.286, f32[128,512]{1,0:T(8,128)S(1)} %fusion.284, f32[128,512]{1,0:T(8,128)S(1)} %fusion.283), kind=kOutput, calls=%fused_computation.2 | convolution fusion | flops 604028928 | bytes 7733252 | tf_op jit(solution)/shard_map/dot_general | solution.py:102
  (210 shorter events, 47.0 us)
Async XLA Ops:
  6.5 12.4 %copy-start = (f32[32,6,512]{2,0,1:T(8,128)S(1)}, f32[32,6,512]{2,0,1:T(8,128)}, u32[]{:S(2)}) copy-start(f32[32,6,512]{2,0,1:T(8,128)} %param.2) | copy-start | bytes 1179652
  6.5 236.2 %all-gather.5.cloned.1.call-start = ((), (), s32[]{:S(2)}) async-start(), calls=%async_computation | async-start | bytes 6684672 | tf_op jit(solution)/shard_map/all_gather | solution.py:89
  6.5 16.4 %collective-permute-start.1 = (f32[32,6,512]{2,0,1:T(8,128)}, f32[32,6,512]{2,0,1:T(8,128)S(1)}, u32[]{:S(2)}, u32[]{:S(2)}) collective-permute-start(f32[32,6,512]{2,0,1:T(8,128)} %param.2), channel_id=1, source_target_pairs={{0,16},{16,32},{32,48},{48,64},{64,80},{80,96},{96,112},{112,128},... | collective-permute-start | bytes 1179656 | tf_op jit(solution)/shard_map/ppermute | solution.py:27
  8.6 14.5 %collective-permute-start = (f32[32,6,512]{2,0,1:T(8,128)}, f32[32,6,512]{2,0,1:T(8,128)S(1)}, u32[]{:S(2)}, u32[]{:S(2)}) collective-permute-start(f32[32,6,512]{2,0,1:T(8,128)} %param.2), channel_id=1, source_target_pairs={{16,0},{32,16},{48,32},{64,48},{80,64},{96,80},{112,96},{128,112},... | collective-permute-start | bytes 1179656 | tf_op jit(solution)/shard_map/ppermute | solution.py:30
  20.7 2.2 copy-start.1
  31.5 7.2 %collective-permute-start.2 = (f32[32,6,512]{2,0,1:T(8,128)S(1)}, f32[32,6,512]{2,0,1:T(8,128)S(1)}, u32[]{:S(2)}, u32[]{:S(2)}) collective-permute-start(f32[32,6,512]{2,0,1:T(8,128)S(1)} %get-tuple-element.21), channel_id=1, source_target_pairs={{16,0},{32,16},{48,32},{64,48},{80,64},{96,80},{112,96},{128,112},... | collective-permute-start | bytes 1179656 | tf_op jit(solution)/shard_map/ppermute | solution.py:30
  33.4 13.7 %collective-permute-start.3 = (f32[32,6,512]{2,0,1:T(8,128)S(1)}, f32[32,6,512]{2,0,1:T(8,128)S(1)}, u32[]{:S(2)}, u32[]{:S(2)}) collective-permute-start(f32[32,6,512]{2,0,1:T(8,128)S(1)} %get-tuple-element.21), channel_id=1, source_target_pairs={{0,16},{16,32},{32,48},{48,64},{64,80},{80,96},{96,112},{112,128},... | collective-permute-start | bytes 1179656 | tf_op jit(solution)/shard_map/ppermute | solution.py:27
  53.7 7.2 %collective-permute-start.4 = (f32[32,6,512]{2,0,1:T(8,128)S(1)}, f32[32,6,512]{2,0,1:T(8,128)S(1)}, u32[]{:S(2)}, u32[]{:S(2)}) collective-permute-start(f32[32,6,512]{2,0,1:T(8,128)S(1)} %fusion.80), channel_id=1, source_target_pairs={{16,0},{32,16},{48,32},{64,48},{80,64},{96,80},{112,96},{128,112},... | collective-permute-start | bytes 1179656 | tf_op jit(solution)/shard_map/ppermute | solution.py:30
  55.6 11.5 %collective-permute-start.5 = (f32[32,6,512]{2,0,1:T(8,128)S(1)}, f32[32,6,512]{2,0,1:T(8,128)S(1)}, u32[]{:S(2)}, u32[]{:S(2)}) collective-permute-start(f32[32,6,512]{2,0,1:T(8,128)S(1)} %fusion.80), channel_id=1, source_target_pairs={{0,16},{16,32},{32,48},{48,64},{64,80},{80,96},{96,112},{112,128},... | collective-permute-start | bytes 1179656 | tf_op jit(solution)/shard_map/ppermute | solution.py:27
  73.7 7.2 %collective-permute-start.6 = (f32[32,6,512]{2,0,1:T(8,128)S(1)}, f32[32,6,512]{2,0,1:T(8,128)S(1)}, u32[]{:S(2)}, u32[]{:S(2)}) collective-permute-start(f32[32,6,512]{2,0,1:T(8,128)S(1)} %fusion.92), channel_id=1, source_target_pairs={{16,0},{32,16},{48,32},{64,48},{80,64},{96,80},{112,96},{128,112},... | collective-permute-start | bytes 1179656 | tf_op jit(solution)/shard_map/ppermute | solution.py:30
  75.7 11.6 %collective-permute-start.7 = (f32[32,6,512]{2,0,1:T(8,128)S(1)}, f32[32,6,512]{2,0,1:T(8,128)S(1)}, u32[]{:S(2)}, u32[]{:S(2)}) collective-permute-start(f32[32,6,512]{2,0,1:T(8,128)S(1)} %fusion.92), channel_id=1, source_target_pairs={{0,16},{16,32},{32,48},{48,64},{64,80},{80,96},{96,112},{112,128},... | collective-permute-start | bytes 1179656 | tf_op jit(solution)/shard_map/ppermute | solution.py:27
  91.7 245.2 %all-gather.9.cloned.1.call-start = ((), (), s32[]{:S(2)}) async-start(), calls=%async_computation.2 | async-start | bytes 2162688 | tf_op jit(solution)/shard_map/all_gather | solution.py:97
  252.0 157.8 %all-gather.7.cloned.1.call-start = ((), (), s32[]{:S(2)}) async-start(), calls=%async_computation.1 | async-start | bytes 1114112 | tf_op jit(solution)/shard_map/all_gather | solution.py:98
Sparse Core Ops, SparseCore 0:
  91.9 150.8 all-gather.4
  252.1 84.7 all-gather.8
  339.5 70.3 all-gather.6
